TPU v7x, 256 devices: a whole 4x4x8 slice. The times are simulated.
256 devices in a mesh: dp: 16 (over x, y), tensor: 16 (over z, core).
Axes of the slice: x: 4, y: 4, z: 8, core: 2. Of those that a mesh axis runs over, the one named last changes fastest.
Arguments:
- tokens: bfloat16 [32768, 1280], P(('dp', 'tensor'))
- cotangent: bfloat16 [32768, 1280], P(('dp', 'tensor')), may hold values from -6 to 6
- gate_weights: float32 [32768, 2], P(('dp', 'tensor')), may hold values from 0.2 to 1
- routes: int32 [32768, 2], P(('dp', 'tensor')), may hold values from 0 to 31, as said below
- slot_index: int32 [32768, 2], P(('dp', 'tensor')), may hold values from -1 to 1, as said below
- qkv_weight: bfloat16 [1280, 16, 240], P(None, 'tensor'), may hold values from -0.15625 to 0.15625
- proj_weight: bfloat16 [16, 80, 1280], P('tensor'), may hold values from -1.25 to 1.25
- up_weight: bfloat16 [32, 1280, 5120], P('dp', None, 'tensor'), may hold values from -0.15625 to 0.15625
- down_weight: bfloat16 [32, 5120, 1280], P('dp', 'tensor'), may hold values from -0.078125 to 0.078125
Outputs:
- layer_out: bfloat16 [32768, 1280], P(('dp', 'tensor'))
- gate_grad: float32 [32768, 2], P(('dp', 'tensor'))
- grad_qkv: float32 [1280, 16, 240], P('dp', 'tensor')
- grad_proj: float32 [16, 80, 1280], P('tensor', None, 'dp')
- grad_up: bfloat16 [32, 1280, 5120], P('dp', None, 'tensor')
- grad_down: bfloat16 [32, 5120, 1280], P('dp', 'tensor')
Inputs may be any that keep to these rules, and one draw needn't show every extreme that they name: `routes`: the two experts of a row differ. `slot_index`: -1 marks a dropped pair; within the rows of one device (aligned blocks of 128 rows) and one expert, the kept pairs hold the slots 0, 1, 2, ... without gaps, each at most once.
All inputs are finite; a program needn't handle non-finite values.
Results may differ from a plain program's by a relative error of at most 0.035.
Values may be sent and summed in bfloat16 or wider, within the bound.
A program may use at most 128 MiB of HBM per device.

v0:
```python
from functools import partial
import math
import jax
import jax.numpy as jnp
from jax import lax
from jax.sharding import PartitionSpec as P

CAP = 2
epsilon = 1e-06
half_root = 1.0 / math.sqrt(2.0)
bell_scale = 1.0 / math.sqrt(2.0 * math.pi)


def norm_parts(row_block):
    widened = row_block.astype(jnp.float32)
    center = widened - jnp.mean(widened, axis=-1, keepdims=True)
    factor = lax.rsqrt(jnp.mean(center * center, axis=-1, keepdims=True) + epsilon)
    return (center * factor, factor)


def norm_back(normal_rows, factor, upstream):
    mean_up = jnp.mean(upstream, axis=-1, keepdims=True)
    mean_mix = jnp.mean(upstream * normal_rows, axis=-1, keepdims=True)
    return factor * (upstream - mean_up - normal_rows * mean_mix)


def gelu_value(pre_act):
    return 0.5 * pre_act * (1.0 + lax.erf(pre_act * half_root))


def gelu_slope(pre_act):
    return (
        0.5 * (1.0 + lax.erf(pre_act * half_root))
        + pre_act * jnp.exp(-0.5 * pre_act * pre_act) * bell_scale
    )


def block_shares(query_block, key_rows, score_scale):
    scores = (
        jnp.einsum("qk,tk->qt", query_block, key_rows, preferred_element_type=jnp.float32)
        * score_scale
    )
    raised = jnp.exp(scores)
    return raised / jnp.sum(raised, axis=-1, keepdims=True)


def attend_head(queries, key_rows, value_rows, block_rows, score_scale):
    block_count = queries.shape[0] // block_rows

    def attend_one_block(query_block):
        shares = block_shares(query_block, key_rows, score_scale)
        context = jnp.dot(
            shares.astype(jnp.bfloat16), value_rows, preferred_element_type=jnp.float32
        )
        return context.astype(jnp.bfloat16)

    outputs = lax.map(attend_one_block, queries.reshape(block_count, block_rows, queries.shape[1]))
    return outputs.reshape(queries.shape)


def head_backward(queries, key_rows, value_rows, grad_context, block_rows, score_scale):
    block_count = queries.shape[0] // block_rows

    def head_one_block(carry, pieces):
        grad_keys, grad_values = carry
        query_block, grad_block = pieces
        shares = block_shares(query_block, key_rows, score_scale)
        grad_shares = jnp.einsum(
            "qk,tk->qt", grad_block, value_rows, preferred_element_type=jnp.float32
        )
        grad_scores = (
            shares
            * (grad_shares - jnp.sum(shares * grad_shares, axis=-1, keepdims=True))
            * score_scale
        ).astype(jnp.bfloat16)
        grad_query = jnp.dot(grad_scores, key_rows, preferred_element_type=jnp.float32).astype(
            jnp.bfloat16
        )
        grad_keys = grad_keys + jnp.einsum(
            "qt,qk->tk", grad_scores, query_block, preferred_element_type=jnp.float32
        )
        grad_values = grad_values + jnp.einsum(
            "qt,qk->tk", shares.astype(jnp.bfloat16), grad_block, preferred_element_type=jnp.float32
        )
        return ((grad_keys, grad_values), grad_query)

    zeros_rows = jnp.zeros(key_rows.shape, jnp.float32)
    shaped = (
        queries.reshape(block_count, block_rows, queries.shape[1]),
        grad_context.reshape(block_count, block_rows, queries.shape[1]),
    )
    (grad_keys, grad_values), grad_queries = lax.scan(
        head_one_block, (zeros_rows, zeros_rows), shaped
    )
    return (
        grad_queries.reshape(queries.shape),
        grad_keys.astype(jnp.bfloat16),
        grad_values.astype(jnp.bfloat16),
    )


def return_slots(expert_partial):
    summed = lax.psum_scatter(
        expert_partial.astype(jnp.bfloat16), "tensor", scatter_dimension=0, tiled=True
    ).astype(jnp.float32)
    returned = lax.all_to_all(
        summed[0].astype(jnp.bfloat16), "dp", split_axis=0, concat_axis=0, tiled=True
    )
    return returned.reshape(
        returned.shape[0] * returned.shape[1] * returned.shape[2], returned.shape[3]
    )


def shards(
    tokens,
    cotangent,
    gate_weights,
    routes,
    slot_index,
    qkv_weight,
    proj_weight,
    up_weight,
    down_weight,
):
    rows_dev, model_width = tokens.shape
    head_size = qkv_weight.shape[2] // 3
    score_scale = head_size ** (-0.5)
    group_count = lax.axis_size("dp")
    local_experts = up_weight.shape[0]
    places = group_count * local_experts * CAP
    normal_in, factor_in = norm_parts(tokens)
    normed = normal_in.astype(jnp.bfloat16)
    full_norm = lax.all_gather(normed, "tensor", axis=0, tiled=True)
    seq_len = full_norm.shape[0]
    block_rows = min(512, seq_len)
    qkv_rows = jnp.einsum(
        "sd,dhc->hsc", full_norm, qkv_weight, preferred_element_type=jnp.float32
    ).astype(jnp.bfloat16)
    queries = qkv_rows[:, :, :head_size]
    key_rows = qkv_rows[:, :, head_size : 2 * head_size]
    value_rows = qkv_rows[:, :, 2 * head_size :]
    context = jax.vmap(partial(attend_head, block_rows=block_rows, score_scale=score_scale))(
        queries, key_rows, value_rows
    )
    attention = lax.psum_scatter(
        jnp.einsum("hsk,hkd->sd", context, proj_weight, preferred_element_type=jnp.float32).astype(
            jnp.bfloat16
        ),
        "tensor",
        scatter_dimension=0,
        tiled=True,
    ).astype(jnp.float32)
    mid = (tokens.astype(jnp.float32) + attention).astype(jnp.bfloat16)
    normal_mid, factor_mid = norm_parts(mid)
    mid_normed = normal_mid.astype(jnp.bfloat16)
    slot_code = jnp.where(slot_index >= 0, routes * CAP + slot_index, -1)
    positions = jnp.arange(places, dtype=jnp.int32)
    pick_both = (slot_code[None, :, :] == positions[:, None, None]).astype(jnp.bfloat16)
    pick_first = pick_both[:, :, 0]
    pick_second = pick_both[:, :, 1]
    dispatch_rows = pick_first + pick_second
    outgoing = jnp.dot(dispatch_rows, mid_normed, preferred_element_type=jnp.float32).astype(
        jnp.bfloat16
    )
    outgoing = outgoing.reshape(group_count, local_experts, CAP, model_width)
    landed = lax.all_to_all(outgoing, "dp", split_axis=0, concat_axis=0, tiled=True)
    arrived = lax.all_gather(landed[None], "tensor", axis=0, tiled=True)
    pre_act = jnp.einsum("tsecd,edf->tsecf", arrived, up_weight, preferred_element_type=jnp.float32)
    hidden = gelu_value(pre_act).astype(jnp.bfloat16)
    expert_partial = jnp.einsum(
        "tsecf,efd->tsecd", hidden, down_weight, preferred_element_type=jnp.float32
    )
    returned = return_slots(expert_partial)
    expert_first = jnp.einsum("pr,pd->rd", pick_first, returned, preferred_element_type=jnp.float32)
    expert_second = jnp.einsum(
        "pr,pd->rd", pick_second, returned, preferred_element_type=jnp.float32
    )
    mixed_rows = gate_weights[:, 0:1] * expert_first + gate_weights[:, 1:2] * expert_second
    layer_out = (mid.astype(jnp.float32) + mixed_rows).astype(jnp.bfloat16)
    upstream = cotangent.astype(jnp.float32)
    gate_grad = jnp.stack(
        [jnp.sum(upstream * expert_first, axis=-1), jnp.sum(upstream * expert_second, axis=-1)],
        axis=1,
    )
    grad_first = (gate_weights[:, 0:1] * upstream).astype(jnp.bfloat16)
    grad_second = (gate_weights[:, 1:2] * upstream).astype(jnp.bfloat16)
    grad_outgoing = jnp.dot(pick_first, grad_first, preferred_element_type=jnp.float32) + jnp.dot(
        pick_second, grad_second, preferred_element_type=jnp.float32
    )
    grad_outgoing = grad_outgoing.astype(jnp.bfloat16).reshape(
        group_count, local_experts, CAP, model_width
    )
    grad_landed = lax.all_to_all(grad_outgoing, "dp", split_axis=0, concat_axis=0, tiled=True)
    grad_arrived = lax.all_gather(grad_landed[None], "tensor", axis=0, tiled=True)
    grad_hidden = jnp.einsum(
        "tsecd,efd->tsecf", grad_arrived, down_weight, preferred_element_type=jnp.float32
    )
    grad_pre = (grad_hidden * gelu_slope(pre_act)).astype(jnp.bfloat16)
    grad_down = jnp.einsum(
        "tsecf,tsecd->efd", hidden, grad_arrived, preferred_element_type=jnp.float32
    ).astype(jnp.bfloat16)
    grad_up = jnp.einsum(
        "tsecd,tsecf->edf", arrived, grad_pre, preferred_element_type=jnp.float32
    ).astype(jnp.bfloat16)
    grad_partial = jnp.einsum(
        "tsecf,edf->tsecd", grad_pre, up_weight, preferred_element_type=jnp.float32
    )
    grad_back = return_slots(grad_partial)
    grad_norm = jnp.einsum(
        "pr,pd->rd", dispatch_rows, grad_back, preferred_element_type=jnp.float32
    )
    grad_mid = (upstream + norm_back(normal_mid, factor_mid, grad_norm)).astype(jnp.bfloat16)
    full_grad = lax.all_gather(grad_mid, "tensor", axis=0, tiled=True)
    grad_context = jnp.einsum(
        "sd,hkd->hsk", full_grad, proj_weight, preferred_element_type=jnp.float32
    ).astype(jnp.bfloat16)
    grad_proj = jnp.einsum("hsk,sd->hkd", context, full_grad, preferred_element_type=jnp.float32)
    grad_queries, grad_keys, grad_values = jax.vmap(
        partial(head_backward, block_rows=block_rows, score_scale=score_scale)
    )(queries, key_rows, value_rows, grad_context)
    grad_rows = jnp.concatenate([grad_queries, grad_keys, grad_values], axis=-1)
    grad_qkv = jnp.einsum("sd,hsc->dhc", full_norm, grad_rows, preferred_element_type=jnp.float32)
    grad_qkv, grad_proj = (
        lax.psum_scatter(
            grad_qkv.astype(jnp.bfloat16), "dp", scatter_dimension=0, tiled=True
        ).astype(jnp.float32),
        lax.psum_scatter(
            grad_proj.astype(jnp.bfloat16), "dp", scatter_dimension=2, tiled=True
        ).astype(jnp.float32),
    )
    return (layer_out, gate_grad, grad_qkv, grad_proj, grad_up, grad_down)


def solution(mesh):
    return jax.shard_map(
        shards,
        mesh=mesh,
        in_specs=(
            P(("dp", "tensor"), None),
            P(("dp", "tensor"), None),
            P(("dp", "tensor"), None),
            P(("dp", "tensor"), None),
            P(("dp", "tensor"), None),
            P(None, "tensor", None),
            P("tensor", None, None),
            P("dp", None, "tensor"),
            P("dp", "tensor", None),
        ),
        out_specs=(
            P(("dp", "tensor"), None),
            P(("dp", "tensor"), None),
            P("dp", "tensor", None),
            P("tensor", None, "dp"),
            P("dp", None, "tensor"),
            P("dp", "tensor", None),
        ),
        check_vma=False,
    )
```

profile of v0, /device:TPU:2, one launch (start us, length us, event | category | flops | bytes accessed | tf_op | source)
XLA Modules:
  0.0 631.2 jit_solution(2711527637385925915)
XLA Ops:
  7.2 1.2 convert_reduce_fusion.1
  8.4 1.2 fusion.86
  9.7 1.9 fusion.87
  11.7 46.4 %all-gather.7.cloned.1.call-done = bf16[2048,1280]{1,0:T(8,128)(2,1)} async-done(((bf16[128,1280]{1,0:T(8,128)(2,1)}), bf16[2048,1280]{1,0:T(8,128)(2,1)}) %all-gather.7.cloned.1.call-update) | async-done | bytes 5242896 | tf_op jit(solution)/shard_map/all_gather | solution.py:133
  58.0 4.2 fusion.47
  62.3 1.0 copy.50
  63.9 8.0 %while.25 = (s32[]{:T(128)}, bf16[4,1,512,80]{2,3,1,0:T(8,128)(2,1)S(1)}, bf16[4,1,512,80]{3,2,1,0:T(8,128)(2,1)S(1)}, bf16[1,2048,80]{2,1,0:T(8,128)(2,1)S(1)}, bf16[1,2048,80]{2,1,0:T(8,128)(2,1)}, /*index=5*/s32[]{:T(128)}) while((s32[]{:T(128)}, bf16[4,1,512,80]{2,3,1,0:T(8,128)(2,1)S(1)}, bf16[4,1,512,80]{3,2,1,0:T(8,128)(2,1)S(1)}, ...), condition=%wide.region_4.5_spmd, body=%wide.region_2.4_spmd.sunk | while | flops 340827648 | bytes 10965105 | solution.py:57
  65.0 0.9 fusion.145
  66.0 0.8 fusion.144
  67.0 0.9 fusion.145
  69.0 0.9 fusion.145
  71.0 0.9 fusion.145
  72.3 3.9 convolution_convert_fusion.1
  77.6 62.2 %reduce-scatter.12.cloned.1.call-done = bf16[128,1280]{1,0:T(8,128)(2,1)} async-done(((bf16[2048,1280]{1,0:T(8,128)(2,1)}), bf16[128,1280]{1,0:T(8,128)(2,1)}) %reduce-scatter.12.cloned.1.call-update) | async-done | bytes 327696 | tf_op jit(solution)/shard_map/reduce_scatter | solution.py:145
  139.7 1.2 convert_reduce_fusion
  141.7 1.7 convolution_convert_fusion.8
  143.4 1.6 reshape.172
  145.1 13.8 %all_to_all.20 = bf16[16,2,2,1280]{3,2,1,0:T(2,128)(2,1)S(1)} all-to-all(bf16[16,2,2,1280]{3,2,1,0:T(2,128)(2,1)} %reshape.172), channel_id=1, replica_groups=mesh['dp'=16,'tensor'=16] {'dp'}, dimensions={0} | all-to-all | bytes 327680 | tf_op jit(solution)/shard_map/all_to_all | solution.py:166
  160.3 1.3 fusion.97
  161.7 1.7 fusion.48
  163.4 1.6 reshape.174
  165.0 11.6 %all_to_all.21 = bf16[16,2,2,1280]{3,2,1,0:T(2,128)(2,1)S(1)} all-to-all(bf16[16,2,2,1280]{3,2,1,0:T(2,128)(2,1)} %reshape.174), channel_id=1, replica_groups=mesh['dp'=16,'tensor'=16] {'dp'}, dimensions={0} | all-to-all | bytes 327680 | tf_op jit(solution)/shard_map/all_to_all | solution.py:193
  177.5 19.0 %all-gather.11.cloned.1.call-done = bf16[256,2,2,1280]{3,0,2,1:T(8,128)(2,1)} async-done(((bf16[16,2,2,1280]{3,0,2,1:T(8,128)(2,1)}), bf16[256,2,2,1280]{3,0,2,1:T(8,128)(2,1)}) %all-gather.11.cloned.1.call-update) | async-done | bytes 2621456 | tf_op jit(solution)/shard_map/all_gather | solution.py:167
  196.6 4.7 fusion.62
  201.2 36.6 %all-gather.13.cloned.1.call-done = bf16[256,2,2,1280]{3,0,2,1:T(8,128)(2,1)} async-done(((bf16[16,2,2,1280]{3,0,2,1:T(8,128)(2,1)}), bf16[256,2,2,1280]{3,0,2,1:T(8,128)(2,1)}) %all-gather.13.cloned.1.call-update) | async-done | bytes 2621456 | tf_op jit(solution)/shard_map/all_gather | solution.py:194
  237.8 4.3 fusion.60
  242.1 0.9 copy-done.10
  243.0 3.0 fusion.38
  246.0 3.0 fusion.37
  250.3 122.9 %all-reduce.9.cloned.1.call-done = (bf16[16,16,2,2,1280]{4,1,3,0,2:T(8,128)(2,1)}, bf16[16,16,2,2,1280]{4,1,3,0,2:T(8,128)(2,1)}) async-done(((bf16[16,16,2,2,1280]{4,1,3,0,2:T(8,128)(2,1)}, bf16[16,16,2,2,1280]{4,1,3,0,2:T(8,128)(2,1)}), (bf16[16,16,2,2,1280]{4,1,3,0,2:T(8,128)(2,1)}, bf16[16,16,2,2,1280]{4,1,3,0,2:T(8,128)(2,1)})) %all-reduce.9.cloned.1.call-update) | async-done | bytes 5242896
  373.2 1.6 dynamic-slice_bitcast_fusion
  375.5 7.3 %all-to-all-start.3 = ((bf16[16,2,2,1280]{3,2,1,0:T(2,128)(2,1)}), bf16[16,2,2,1280]{3,2,1,0:T(2,128)(2,1)S(1)}, u32[]{:S(2)}, u32[]{:S(2)}) async-start(bf16[16,2,2,1280]{3,2,1,0:T(2,128)(2,1)} %copy.57), calls=%async_computation.4 | async-start | bytes 327680 | tf_op jit(solution)/shard_map/all_to_all | solution.py:106
  382.8 1.6 dynamic-slice_bitcast_fusion.1
  385.2 4.1 all-to-all-done.3
  389.3 5.1 all-to-all-start.1
  394.6 1.9 fusion.114
  396.5 4.4 all-to-all-done.1
  401.3 3.0 fusion.90
  404.4 1.3 dynamic-slice.4
  406.3 4.0 fusion.40
  410.2 35.1 %all-gather.9.cloned.1.call-done = bf16[2048,1280]{1,0:T(8,128)(2,1)} async-done(((bf16[128,1280]{1,0:T(8,128)(2,1)}), bf16[2048,1280]{1,0:T(8,128)(2,1)}) %all-gather.9.cloned.1.call-update) | async-done | bytes 5242896 | tf_op jit(solution)/shard_map/all_gather | solution.py:213
  445.3 4.2 fusion.50
  449.8 4.2 fusion.49
  454.0 1.0 copy.72
  455.1 23.7 %while.26 = (s32[]{:T(128)}, f32[1,2048,80]{1,2,0:T(8,128)S(1)}, f32[1,2048,80]{1,2,0:T(8,128)S(1)}, bf16[4,1,512,80]{2,3,1,0:T(8,128)(2,1)S(1)}, bf16[4,1,512,8...) while((s32[]{:T(128)}, f32[1,2048,80]{1,2,0:T(8,128)S(1)}, ...), condition=%wide.region_17.18_spmd.clone, body=%wide.region_14.17_spmd.clone.sunk | while | flops 855284736 | bytes 37580964 | solution.py:92
  456.2 0.9 fusion.154
  457.1 1.4 multiply_reduce_fusion.2
  458.5 1.1 multiply_convert_fusion.2
  462.1 0.9 fusion.154
  463.0 1.4 multiply_reduce_fusion.2
  464.4 1.1 multiply_convert_fusion.2
  468.0 0.9 fusion.154
  468.9 1.4 multiply_reduce_fusion.2
  470.4 1.1 multiply_convert_fusion.2
  473.9 1.0 fusion.154
  474.9 1.4 multiply_reduce_fusion.2
  476.3 1.1 multiply_convert_fusion.2
  478.9 4.0 convolution_convert_fusion.4
  482.9 1.1 copy.82
  484.0 4.1 fusion.39
  488.7 52.8 %all-reduce.7.cloned.1.call-done = bf16[1,80,1280]{2,1,0:T(8,128)(2,1)} async-done(((bf16[1,80,1280]{2,1,0:T(8,128)(2,1)}), bf16[1,80,1280]{2,1,0:T(8,128)(2,1)}) %all-reduce.7.cloned.1.call-update) | async-done | bytes 204816
  541.5 1.5 dynamic-slice_convert_fusion
  543.0 79.8 %reduce-scatter.14.cloned.1.call-done = bf16[80,240]{1,0:T(8,128)(2,1)} async-done(((bf16[1280,240]{1,0:T(8,128)(2,1)}), bf16[80,240]{1,0:T(8,128)(2,1)}) %reduce-scatter.14.cloned.1.call-update) | async-done | bytes 38416
  622.7 0.9 copy.83
  (126 shorter events, 23.7 us)
Async XLA Ops:
  7.2 189.4 %copy-start = (bf16[2,1280,320]{1,2,0:T(8,128)(2,1)S(1)}, bf16[2,1280,320]{1,2,0:T(8,128)(2,1)}, u32[]{:S(2)}) copy-start(bf16[2,1280,320]{1,2,0:T(8,128)(2,1)} %param.20) | copy-start | bytes 4915204
  7.2 50.8 %all-gather.7.cloned.1.call-start = ((), (), s32[]{:S(2)}) async-start(), calls=%async_computation.6 | async-start | bytes 5570560 | tf_op jit(solution)/shard_map/all_gather | solution.py:133
  11.6 128.1 %reduce-scatter.12.cloned.1.call-start = ((), (), s32[]{:S(2)}) async-start(), calls=%async_computation.7 | async-start | bytes 5570560 | tf_op jit(solution)/shard_map/reduce_scatter | solution.py:145
  63.9 8.4 %copy-start.7 = (bf16[1,80,1280]{2,1,0:T(8,128)(2,1)S(1)}, bf16[1,80,1280]{2,1,0:T(8,128)(2,1)}, u32[]{:S(2)}) copy-start(bf16[1,80,1280]{2,1,0:T(8,128)(2,1)} %param.19) | copy-start | bytes 614404
  63.9 1.1 copy-start.13
  66.0 1.0 copy-start.13
  68.0 1.0 copy-start.13
  70.0 1.0 copy-start.13
  76.2 0.7 copy-start.19
  76.2 0.7 copy-start.20
  76.2 63.5 %copy-start.2 = (bf16[128,1280]{1,0:T(8,128)(2,1)S(1)}, bf16[128,1280]{1,0:T(8,128)(2,1)}, u32[]{:S(2)}) copy-start(bf16[128,1280]{1,0:T(8,128)(2,1)} %param.13) | copy-start | bytes 983044
  76.3 120.3 %all-gather.11.cloned.1.call-start = ((), (), s32[]{:S(2)}) async-start(), calls=%async_computation.9 | async-start | bytes 2785280 | tf_op jit(solution)/shard_map/all_gather | solution.py:167
  140.9 0.7 copy-start.3
  140.9 20.8 %copy-start.6 = (bf16[128,1280]{1,0:T(8,128)(2,1)S(1)}, bf16[128,1280]{1,0:T(8,128)(2,1)}, u32[]{:S(2)}) copy-start(bf16[128,1280]{1,0:T(8,128)(2,1)} %param.14) | copy-start | bytes 983044
  141.2 0.5 copy-start.21
  159.5 78.3 %all-gather.13.cloned.1.call-start = ((), (), s32[]{:S(2)}) async-start(), calls=%async_computation.10 | async-start | bytes 2785280 | tf_op jit(solution)/shard_map/all_gather | solution.py:194
  160.3 1.3 copy-start.17
  177.3 195.9 %all-reduce.9.cloned.1.call-start = ((), (), s32[]{:S(2)}) async-start(), calls=%async_computation.13 | async-start | bytes 10485760
  242.1 0.9 copy-start.10
  243.0 3.0 copy-start.5
  243.0 3.0 copy-start.8
  249.0 0.7 copy-start.25
  249.0 145.5 %copy-start.4 = (bf16[128,1280]{1,0:T(8,128)(2,1)S(1)}, bf16[128,1280]{1,0:T(8,128)(2,1)}, u32[]{:S(2)}) copy-start(bf16[128,1280]{1,0:T(8,128)(2,1)} %copy-done.3) | copy-start | bytes 983044
  249.0 145.5 %copy-start.22 = (f32[128]{0:T(128)S(1)}, f32[128]{0:T(128)}, u32[]{:S(2)}) copy-start(f32[128]{0:T(128)} %copy-done.21) | copy-start | bytes 1540
  249.1 151.9 %copy-start.16 = (pred[64,128,2]{1,0,2:T(32,128)(4,1)S(1)}, pred[64,128,2]{1,0,2:T(32,128)(4,1)}, u32[]{:S(2)}) copy-start(pred[64,128,2]{1,0,2:T(32,128)(4,1)} %get-tuple-element.212) | copy-start | bytes 49156
  249.1 152.2 %copy-start.18 = (f32[128]{0:T(128)S(1)}, f32[128]{0:T(128)}, u32[]{:S(2)}) copy-start(f32[128]{0:T(128)} %copy-done.17) | copy-start | bytes 1540
  375.5 13.7 %all-to-all-start.3 = ((bf16[16,2,2,1280]{3,2,1,0:T(2,128)(2,1)}), bf16[16,2,2,1280]{3,2,1,0:T(2,128)(2,1)S(1)}, u32[]{:S(2)}, u32[]{:S(2)}) async-start(bf16[16,2,2,1280]{3,2,1,0:T(2,128)(2,1)} %copy.57), calls=%async_computation.4 | async-start | bytes 327680 | tf_op jit(solution)/shard_map/all_to_all | solution.py:106
  389.3 11.6 %all-to-all-start.1 = ((bf16[16,2,2,1280]{3,2,1,0:T(2,128)(2,1)}), bf16[16,2,2,1280]{3,2,1,0:T(2,128)(2,1)S(1)}, u32[]{:S(2)}, u32[]{:S(2)}) async-start(bf16[16,2,2,1280]{3,2,1,0:T(2,128)(2,1)} %copy.54), calls=%async_computation.2 | async-start | bytes 327680 | tf_op jit(solution)/shard_map/all_to_all | solution.py:106
  394.4 50.9 %all-gather.9.cloned.1.call-start = ((), (), s32[]{:S(2)}) async-start(), calls=%async_computation.8 | async-start | bytes 5570560 | tf_op jit(solution)/shard_map/all_gather | solution.py:213
  394.6 11.7 %copy-start.11 = (bf16[16,16,2,2,320]{4,1,3,0,2:T(8,128)(2,1)S(1)}, bf16[16,16,2,2,320]{4,1,3,0,2:T(8,128)(2,1)}, u32[]{:S(2)}) copy-start(bf16[16,16,2,2,320]{4,1,3,0,2:T(8,128)(2,1)} %copy-done.10) | copy-start | bytes 1966084
  404.3 137.2 %all-reduce.7.cloned.1.call-start = ((), (), s32[]{:S(2)}) async-start(), calls=%async_computation.12 | async-start | bytes 409600
  449.5 5.6 copy-start.12
  449.5 5.6 copy-start.14
  449.5 173.2 %reduce-scatter.14.cloned.1.call-start = ((), (), s32[]{:S(2)}) async-start(), calls=%async_computation.11 | async-start | bytes 696320
  455.1 1.0 copy-start.15
  461.0 1.0 copy-start.15
  466.9 1.0 copy-start.15
  472.9 1.0 copy-start.15
  478.9 5.1 copy-start.9
  484.0 4.1 copy-start.23
  484.0 4.1 copy-start.24
  484.0 140.4 %copy-start.1 = (bf16[2,1280,320]{1,2,0:T(8,128)(2,1)S(1)}, bf16[2,1280,320]{1,2,0:T(8,128)(2,1)}, u32[]{:S(2)}) copy-start(bf16[2,1280,320]{1,2,0:T(8,128)(2,1)} %param.20) | copy-start | bytes 4915204
Sparse Core Ops, SparseCore 0:
  11.7 46.2 all-gather.6
  76.4 63.3 reduce-scatter.11
  159.6 36.8 all-gather.10
  198.8 38.9 all-gather.12
  249.2 123.9 all-reduce.8
  404.4 40.8 all-gather.8
  449.6 91.7 all-reduce.6
  545.4 77.3 reduce-scatter.13
where the time goes:
time: 633 us; the launch traced here: 631 us
  waiting for transfers between devices  463 us (73%)
  matrix products  78.8 us (12%)
  blocking collectives  25.4 us (4%)
  local copies, waits for them, and re-layouts  22.2 us (4%)
  between operations  15.2 us (2%)
  starting transfers between devices  13.1 us (2%)
  other arithmetic  13 us (2%)
    unnamed x11, waiting for transfers between devices  256 us
    reduce_scatter x1, waiting for transfers between devices, shards(): lax.psum_scatter(jnp.einsum('hsk,hkd->sd', context, proj_weight, preferre...  62.2 us
    all_gather x1, waiting for transfers between devices, shards(): full_norm = lax.all_gather(normed, 'tensor', axis=0, tiled=True)  46.4 us
    all_gather x1, waiting for transfers between devices, shards(): lax.all_gather(grad_landed[None], 'tensor', axis=0, tiled=True)  36.6 us
    all_gather x1, waiting for transfers between devices, shards(): full_grad = lax.all_gather(grad_mid, 'tensor', axis=0, tiled=True)  35.1 us
    all_gather x1, waiting for transfers between devices, shards(): arrived = lax.all_gather(landed[None], 'tensor', axis=0, tiled=True)  19 us
    all_to_all x1, blocking collectives, shards(): lax.all_to_all(outgoing, 'dp', split_axis=0, concat_axis=0, tiled=True)  13.8 us
  transfers between devices with their start and end apart: 10, of which 10 were waited for; matrix products, arithmetic and copies ran while one was open for 10% of the time, Pallas kernels for 0%

commit v1 on v0

--- a/solution.py
+++ b/solution.py
@@ -122,6 +122,20 @@
     up_weight,
     down_weight,
 ):
+
+    def store_boxes(work_x):
+        shard_axis = "tensor"
+        n_chips = lax.axis_size(shard_axis)
+        xs_all = tuple(((u, (u + 1) % n_chips) for u in range(n_chips)))
+        then, even = ([work_x], [work_x])
+        items = tuple(((u, (u - 1) % n_chips) for u in range(n_chips)))
+        for _ in range(n_chips // 2):
+            then.append(lax.ppermute(then[-1], shard_axis, xs_all))
+        for _ in range((n_chips - 1) // 2):
+            even.append(lax.ppermute(even[-1], shard_axis, items))
+        o_now = jnp.concatenate([*then[::-1], *even[1:]], 0)
+        return jnp.roll(o_now, (lax.axis_index(shard_axis) - n_chips // 2) * work_x.shape[0], 0)
+
     rows_dev, model_width = tokens.shape
     head_size = qkv_weight.shape[2] // 3
     score_scale = head_size ** (-0.5)
@@ -130,7 +144,7 @@
     places = group_count * local_experts * CAP
     normal_in, factor_in = norm_parts(tokens)
     normed = normal_in.astype(jnp.bfloat16)
-    full_norm = lax.all_gather(normed, "tensor", axis=0, tiled=True)
+    full_norm = store_boxes(normed)
     seq_len = full_norm.shape[0]
     block_rows = min(512, seq_len)
     qkv_rows = jnp.einsum(

time: 633 us -> 664 us (1.049)
  starting transfers between devices: 13.1 us -> 34.2 us
  waiting for transfers between devices: 463 us -> 444 us
  local copies, waits for them, and re-layouts: 22.2 us -> 38.3 us
  matrix products: 78.8 us -> 91.6 us
    all_gather x1 -> x0, waiting for transfers between devices: 46.4 us -> none  [shards(): full_norm = lax.all_gather(normed, 'tensor', axis=0, tiled=True)]
    ppermute x0 -> x15, waiting for transfers between devices: none -> 42.5 us  [the longest x8 41.1 us: store_boxes(): then.append(lax.ppermute(then[-1], shard_axis, xs_all))]
    unnamed x11 -> x10, waiting for transfers between devices: 256 us -> 233 us
    ppermute x0 -> x15, starting transfers between devices: none -> 21.1 us  [the longest x7 21.1 us: store_boxes(): even.append(lax.ppermute(even[-1], shard_axis, items))]
    unnamed x55 -> x102, local copies, waits for them, and re-layouts: 8.34 us -> 22.1 us
    dot_general x4, matrix products: 3.8 us -> 11.8 us  [head_one_block(): jnp.einsum('qt,qk->tk', shares.astype(jnp.bfloat16), grad_block, preferre...]
  transfers between devices with their start and end apart: 10 -> 24, of which waited for: 10 -> 19; matrix products, arithmetic and copies ran while one was open for 10% -> 13% of each run, Pallas kernels for 0% -> 0%
where the time goes in v1:
time: 664 us; the launch traced here: 662 us
  waiting for transfers between devices  444 us (67%)
  matrix products  91.6 us (14%)
  local copies, waits for them, and re-layouts  38.3 us (6%)
  starting transfers between devices  34.2 us (5%)
  blocking collectives  25 us (4%)
  between operations  15.5 us (2%)
  other arithmetic  13.1 us (2%)
    unnamed x10, waiting for transfers between devices  233 us
    reduce_scatter x1, waiting for transfers between devices, shards(): lax.psum_scatter(jnp.einsum('hsk,hkd->sd', context, proj_weight, preferre...  64.9 us
    ppermute x8, waiting for transfers between devices, store_boxes(): then.append(lax.ppermute(then[-1], shard_axis, xs_all))  41.1 us
    all_gather x1, waiting for transfers between devices, shards(): lax.all_gather(grad_landed[None], 'tensor', axis=0, tiled=True)  36.7 us
    all_gather x1, waiting for transfers between devices, shards(): full_grad = lax.all_gather(grad_mid, 'tensor', axis=0, tiled=True)  35.7 us
    unnamed x102, local copies, waits for them, and re-layouts  22.1 us
    ppermute x7, starting transfers between devices, store_boxes(): even.append(lax.ppermute(even[-1], shard_axis, items))  21.1 us
    all_gather x1, waiting for transfers between devices, shards(): arrived = lax.all_gather(landed[None], 'tensor', axis=0, tiled=True)  20.4 us
  transfers between devices with their start and end apart: 24, of which 19 were waited for; matrix products, arithmetic and copies ran while one was open for 13% of the time, Pallas kernels for 0%

profile of v1, /device:TPU:2, one launch (start us, length us, event | category | flops | bytes accessed | tf_op | source)
XLA Modules:
  0.0 661.8 jit_solution(13883709570388416000)
XLA Ops:
  10.9 10.0 %collective-permute-done = bf16[128,1280]{1,0:T(8,128)(2,1)S(1)} collective-permute-done((bf16[128,1280]{1,0:T(8,128)(2,1)S(1)}, bf16[128,1280]{1,0:T(8,128)(2,1)S(1)}, u32[]{:S(2)}, u32[]{:S(2)}) %collective-permute-start) | collective-permute-done | bytes 327712 | tf_op jit(solution)/shard_map/ppermute | solution.py:133
  21.0 3.0 collective-permute-start.8
  23.9 4.8 collective-permute-done.1
  28.7 3.0 collective-permute-start.9
  31.7 4.7 collective-permute-done.2
  36.4 3.0 collective-permute-start.10
  39.4 4.7 collective-permute-done.3
  44.2 2.9 collective-permute-start.11
  47.1 4.7 collective-permute-done.4
  52.6 2.9 collective-permute-start.12
  55.5 4.0 collective-permute-done.5
  60.1 3.2 collective-permute-start.13
  63.3 4.0 collective-permute-done.6
  68.3 3.1 collective-permute-start.14
  71.4 4.0 collective-permute-done.7
  88.6 1.6 fusion.57
  90.2 2.4 copy-done.32
  96.0 8.1 %while.25 = (s32[]{:T(128)}, bf16[4,1,512,80]{2,3,1,0:T(8,128)(2,1)S(1)}, bf16[4,1,512,80]{3,2,1,0:T(8,128)(2,1)S(1)}, bf16[1,2048,80]{2,1,0:T(8,128)(2,1)S(1)}, bf16[1,2048,80]{2,1,0:T(8,128)(2,1)}, /*index=5*/s32[]{:T(128)}) while((s32[]{:T(128)}, bf16[4,1,512,80]{2,3,1,0:T(8,128)(2,1)S(1)}, bf16[4,1,512,80]{3,2,1,0:T(8,128)(2,1)S(1)}, ...), condition=%wide.region_4.5_spmd, body=%wide.region_2.4_spmd.sunk | while | flops 340827648 | bytes 10965097 | solution.py:57
  105.2 4.8 convolution_convert_fusion.1
  110.6 64.9 %reduce-scatter.12.cloned.1.call-done = bf16[128,1280]{1,0:T(8,128)(2,1)} async-done(((bf16[2048,1280]{1,0:T(8,128)(2,1)}), bf16[128,1280]{1,0:T(8,128)(2,1)}) %reduce-scatter.12.cloned.1.call-update) | async-done | bytes 327696 | tf_op jit(solution)/shard_map/reduce_scatter | solution.py:159
  177.3 13.5 %all_to_all.20 = bf16[16,2,2,1280]{3,2,1,0:T(2,128)(2,1)S(1)} all-to-all(bf16[16,2,2,1280]{3,2,1,0:T(2,128)(2,1)S(1)} %reshape.172), channel_id=1, replica_groups=mesh['dp'=16,'tensor'=16] {'dp'}, dimensions={0} | all-to-all | bytes 327680 | tf_op jit(solution)/shard_map/all_to_all | solution.py:180
  192.9 1.9 fusion.60
  195.8 11.4 %all_to_all.21 = bf16[16,2,2,1280]{3,2,1,0:T(2,128)(2,1)S(1)} all-to-all(bf16[16,2,2,1280]{3,2,1,0:T(2,128)(2,1)S(1)} %reshape.174), channel_id=1, replica_groups=mesh['dp'=16,'tensor'=16] {'dp'}, dimensions={0} | all-to-all | bytes 327680 | tf_op jit(solution)/shard_map/all_to_all | solution.py:207
  208.2 20.4 %all-gather.8.cloned.1.call-done = bf16[256,2,2,1280]{3,0,2,1:T(8,128)(2,1)} async-done(((bf16[16,2,2,1280]{3,0,2,1:T(8,128)(2,1)}), bf16[256,2,2,1280]{3,0,2,1:T(8,128)(2,1)}) %all-gather.8.cloned.1.call-update) | async-done | bytes 2621456 | tf_op jit(solution)/shard_map/all_gather | solution.py:181
  228.6 4.7 fusion.74
  233.3 36.7 %all-gather.10.cloned.1.call-done = bf16[256,2,2,1280]{3,0,2,1:T(8,128)(2,1)} async-done(((bf16[16,2,2,1280]{3,0,2,1:T(8,128)(2,1)}), bf16[256,2,2,1280]{3,0,2,1:T(8,128)(2,1)}) %all-gather.10.cloned.1.call-update) | async-done | bytes 2621456 | tf_op jit(solution)/shard_map/all_gather | solution.py:208
  270.0 4.3 fusion.72
  275.2 3.1 fusion.42
  278.3 3.1 fusion.41
  282.0 123.5 %all-reduce.9.cloned.1.call-done = (bf16[16,16,2,2,1280]{4,1,3,0,2:T(8,128)(2,1)}, bf16[16,16,2,2,1280]{4,1,3,0,2:T(8,128)(2,1)}) async-done(((bf16[16,16,2,2,1280]{4,1,3,0,2:T(8,128)(2,1)}, bf16[16,16,2,2,1280]{4,1,3,0,2:T(8,128)(2,1)}), (bf16[16,16,2,2,1280]{4,1,3,0,2:T(8,128)(2,1)}, bf16[16,16,2,2,1280]{4,1,3,0,2:T(8,128)(2,1)})) %all-reduce.9.cloned.1.call-update) | async-done | bytes 5242896
  405.5 1.6 dynamic-slice_bitcast_fusion
  407.8 7.3 %all-to-all-start.3 = ((bf16[16,2,2,1280]{3,2,1,0:T(2,128)(2,1)}), bf16[16,2,2,1280]{3,2,1,0:T(2,128)(2,1)S(1)}, u32[]{:S(2)}, u32[]{:S(2)}) async-start(bf16[16,2,2,1280]{3,2,1,0:T(2,128)(2,1)} %copy.57), calls=%async_computation.4 | async-start | bytes 327680 | tf_op jit(solution)/shard_map/all_to_all | solution.py:106
  415.1 1.6 dynamic-slice_bitcast_fusion.1
  417.5 4.1 all-to-all-done.3
  421.6 5.1 all-to-all-start.1
  427.2 6.0 all-to-all-done.1
  436.3 4.0 fusion.44
  440.3 35.7 %all-gather.6.cloned.1.call-done = bf16[2048,1280]{1,0:T(8,128)(2,1)} async-done(((bf16[128,1280]{1,0:T(8,128)(2,1)}), bf16[2048,1280]{1,0:T(8,128)(2,1)}) %all-gather.6.cloned.1.call-update) | async-done | bytes 5242896 | tf_op jit(solution)/shard_map/all_gather | solution.py:227
  476.0 4.2 fusion.62
  480.5 4.2 fusion.61
  485.7 44.4 %while.26 = (s32[]{:T(128)}, f32[1,2048,80]{1,2,0:T(8,128)S(1)}, f32[1,2048,80]{1,2,0:T(8,128)}, bf16[4,1,512,80]{2,3,1,0:T(8,128)(2,1)}, bf16[4,1,512,80]{3,2,1...) while((s32[]{:T(128)}, f32[1,2048,80]{1,2,0:T(8,128)S(1)}, ...), condition=%wide.region_17.18_spmd.clone, body=%wide.region_14.17_spmd.clone.sunk | while | flops 855284736 | bytes 73365768 | solution.py:92
  485.7 1.9 fusion.164
  487.6 1.4 multiply_reduce_fusion.2
  490.8 1.6 fusion.165
  492.4 1.4 fusion.167
  493.8 2.8 fusion.166
  496.6 1.9 fusion.164
  498.5 1.4 multiply_reduce_fusion.2
  501.7 1.6 fusion.165
  503.3 1.4 fusion.167
  504.7 3.0 fusion.166
  507.7 1.9 fusion.164
  512.8 1.6 fusion.165
  514.5 1.4 fusion.167
  515.9 3.0 fusion.166
  518.9 1.9 fusion.164
  524.0 1.6 fusion.165
  525.6 1.4 fusion.167
  527.0 3.0 fusion.166
  532.2 4.0 fusion.54
  537.4 4.1 fusion.43
  542.1 30.0 %all-reduce.7.cloned.1.call-done = bf16[1,80,1280]{2,1,0:T(8,128)(2,1)} async-done(((bf16[1,80,1280]{2,1,0:T(8,128)(2,1)}), bf16[1,80,1280]{2,1,0:T(8,128)(2,1)}) %all-reduce.7.cloned.1.call-update) | async-done | bytes 204816
  572.1 1.5 dynamic-slice_convert_fusion
  573.5 79.8 %reduce-scatter.14.cloned.1.call-done = bf16[80,240]{1,0:T(8,128)(2,1)} async-done(((bf16[1280,240]{1,0:T(8,128)(2,1)}), bf16[80,240]{1,0:T(8,128)(2,1)}) %reduce-scatter.14.cloned.1.call-update) | async-done | bytes 38416
  (235 shorter events, 60.1 us)
Async XLA Ops:
  7.2 221.4 %copy-start = (bf16[2,1280,320]{1,2,0:T(8,128)(2,1)S(1)}, bf16[2,1280,320]{1,2,0:T(8,128)(2,1)}, u32[]{:S(2)}) copy-start(bf16[2,1280,320]{1,2,0:T(8,128)(2,1)} %param.20) | copy-start | bytes 4915204
  7.2 74.4 %copy-start.5 = (bf16[128,1280]{1,0:T(8,128)(2,1)S(1)}, bf16[128,1280]{1,0:T(8,128)(2,1)}, u32[]{:S(2)}) copy-start(bf16[128,1280]{1,0:T(8,128)(2,1)} %param.13) | copy-start | bytes 983044
  7.2 168.4 %reduce-scatter.12.cloned.1.call-start = ((), (), s32[]{:S(2)}) async-start(), calls=%async_computation.6 | async-start | bytes 5570560 | tf_op jit(solution)/shard_map/reduce_scatter | solution.py:159
  10.9 10.1 %collective-permute-start = (bf16[128,1280]{1,0:T(8,128)(2,1)S(1)}, bf16[128,1280]{1,0:T(8,128)(2,1)S(1)}, u32[]{:S(2)}, u32[]{:S(2)}) collective-permute-start(bf16[128,1280]{1,0:T(8,128)(2,1)S(1)} %fusion.99), channel_id=1, source_target_pairs={{0,1},{1,2},{2,3},{3,4},{4,5},{5,6},{6,7},{7,8},{8,9},{9,10},{10,1... | collective-permute-start | bytes 983048 | tf_op jit(solution)/shard_map/ppermute | solution.py:133
  21.0 7.7 %collective-permute-start.1 = (bf16[128,1280]{1,0:T(8,128)(2,1)S(1)}, bf16[128,1280]{1,0:T(8,128)(2,1)S(1)}, u32[]{:S(2)}, u32[]{:S(2)}) collective-permute-start(bf16[128,1280]{1,0:T(8,128)(2,1)S(1)} %collective-permute-done), channel_id=1, source_target_pairs={{0,1},{1,2},{2,3},{3,4},{4,5},{5,6},{6,7},{7,8},{8,9},{9,10},{10,1... | collective-permute-start | bytes 983048 | tf_op jit(solution)/shard_map/ppermute | solution.py:133
  21.0 7.7 %collective-permute-start.8 = (bf16[128,1280]{1,0:T(8,128)(2,1)S(1)}, bf16[128,1280]{1,0:T(8,128)(2,1)S(1)}, u32[]{:S(2)}, u32[]{:S(2)}) collective-permute-start(bf16[128,1280]{1,0:T(8,128)(2,1)S(1)} %fusion.99), channel_id=1, source_target_pairs={{0,15},{1,0},{2,1},{3,2},{4,3},{5,4},{6,5},{7,6},{8,7},{9,8},{10,9... | collective-permute-start | bytes 983048 | tf_op jit(solution)/shard_map/ppermute | solution.py:135
  28.7 7.7 %collective-permute-start.2 = (bf16[128,1280]{1,0:T(8,128)(2,1)S(1)}, bf16[128,1280]{1,0:T(8,128)(2,1)S(1)}, u32[]{:S(2)}, u32[]{:S(2)}) collective-permute-start(bf16[128,1280]{1,0:T(8,128)(2,1)S(1)} %collective-permute-done.1), channel_id=1, source_target_pairs={{0,1},{1,2},{2,3},{3,4},{4,5},{5,6},{6,7},{7,8},{8,9},{9,10},{10,1... | collective-permute-start | bytes 983048 | tf_op jit(solution)/shard_map/ppermute | solution.py:133
  28.7 7.7 %collective-permute-start.9 = (bf16[128,1280]{1,0:T(8,128)(2,1)S(1)}, bf16[128,1280]{1,0:T(8,128)(2,1)S(1)}, u32[]{:S(2)}, u32[]{:S(2)}) collective-permute-start(bf16[128,1280]{1,0:T(8,128)(2,1)S(1)} %collective-permute-done.8), channel_id=1, source_target_pairs={{0,15},{1,0},{2,1},{3,2},{4,3},{5,4},{6,5},{7,6},{8,7},{9,8},{10,9... | collective-permute-start | bytes 983048 | tf_op jit(solution)/shard_map/ppermute | solution.py:135
  36.4 7.7 %copy-start.10 = (bf16[128,1280]{1,0:T(8,128)(2,1)}, bf16[128,1280]{1,0:T(8,128)(2,1)S(1)}, u32[]{:S(2)}) copy-start(bf16[128,1280]{1,0:T(8,128)(2,1)S(1)} %collective-permute-done.2) | copy-start | bytes 983044
  36.4 7.7 %collective-permute-start.3 = (bf16[128,1280]{1,0:T(8,128)(2,1)S(1)}, bf16[128,1280]{1,0:T(8,128)(2,1)S(1)}, u32[]{:S(2)}, u32[]{:S(2)}) collective-permute-start(bf16[128,1280]{1,0:T(8,128)(2,1)S(1)} %collective-permute-done.2), channel_id=1, source_target_pairs={{0,1},{1,2},{2,3},{3,4},{4,5},{5,6},{6,7},{7,8},{8,9},{9,10},{10,1... | collective-permute-start | bytes 983048 | tf_op jit(solution)/shard_map/ppermute | solution.py:133
  36.4 7.7 %collective-permute-start.10 = (bf16[128,1280]{1,0:T(8,128)(2,1)S(1)}, bf16[128,1280]{1,0:T(8,128)(2,1)S(1)}, u32[]{:S(2)}, u32[]{:S(2)}) collective-permute-start(bf16[128,1280]{1,0:T(8,128)(2,1)S(1)} %collective-permute-done.9), channel_id=1, source_target_pairs={{0,15},{1,0},{2,1},{3,2},{4,3},{5,4},{6,5},{7,6},{8,7},{9,8},{10,9... | collective-permute-start | bytes 983048 | tf_op jit(solution)/shard_map/ppermute | solution.py:135
  44.1 16.0 %copy-start.16 = (bf16[128,1280]{1,0:T(8,128)(2,1)}, bf16[128,1280]{1,0:T(8,128)(2,1)S(1)}, u32[]{:S(2)}) copy-start(bf16[128,1280]{1,0:T(8,128)(2,1)S(1)} %collective-permute-done.3) | copy-start | bytes 983044
  44.1 7.7 %collective-permute-start.4 = (bf16[128,1280]{1,0:T(8,128)(2,1)S(1)}, bf16[128,1280]{1,0:T(8,128)(2,1)S(1)}, u32[]{:S(2)}, u32[]{:S(2)}) collective-permute-start(bf16[128,1280]{1,0:T(8,128)(2,1)S(1)} %collective-permute-done.3), channel_id=1, source_target_pairs={{0,1},{1,2},{2,3},{3,4},{4,5},{5,6},{6,7},{7,8},{8,9},{9,10},{10,1... | collective-permute-start | bytes 983048 | tf_op jit(solution)/shard_map/ppermute | solution.py:133
  44.2 7.7 %collective-permute-start.11 = (bf16[128,1280]{1,0:T(8,128)(2,1)S(1)}, bf16[128,1280]{1,0:T(8,128)(2,1)S(1)}, u32[]{:S(2)}, u32[]{:S(2)}) collective-permute-start(bf16[128,1280]{1,0:T(8,128)(2,1)S(1)} %collective-permute-done.10), channel_id=1, source_target_pairs={{0,15},{1,0},{2,1},{3,2},{4,3},{5,4},{6,5},{7,6},{8,7},{9,8},{10,9... | collective-permute-start | bytes 983048 | tf_op jit(solution)/shard_map/ppermute | solution.py:135
  51.8 11.5 %copy-start.18 = (bf16[128,1280]{1,0:T(8,128)(2,1)}, bf16[128,1280]{1,0:T(8,128)(2,1)S(1)}, u32[]{:S(2)}) copy-start(bf16[128,1280]{1,0:T(8,128)(2,1)S(1)} %collective-permute-done.4) | copy-start | bytes 983044
  51.8 7.7 %collective-permute-start.5 = (bf16[128,1280]{1,0:T(8,128)(2,1)S(1)}, bf16[128,1280]{1,0:T(8,128)(2,1)S(1)}, u32[]{:S(2)}, u32[]{:S(2)}) collective-permute-start(bf16[128,1280]{1,0:T(8,128)(2,1)S(1)} %collective-permute-done.4), channel_id=1, source_target_pairs={{0,1},{1,2},{2,3},{3,4},{4,5},{5,6},{6,7},{7,8},{8,9},{9,10},{10,1... | collective-permute-start | bytes 983048 | tf_op jit(solution)/shard_map/ppermute | solution.py:133
  52.6 7.5 %collective-permute-start.12 = (bf16[128,1280]{1,0:T(8,128)(2,1)S(1)}, bf16[128,1280]{1,0:T(8,128)(2,1)}, u32[]{:S(2)}, u32[]{:S(2)}) collective-permute-start(bf16[128,1280]{1,0:T(8,128)(2,1)S(1)} %collective-permute-done.11), channel_id=1, source_target_pairs={{0,15},{1,0},{2,1},{3,2},{4,3},{5,4},{6,5},{7,6},{8,7},{9,8},{10,9... | collective-permute-start | bytes 983048 | tf_op jit(solution)/shard_map/ppermute | solution.py:135
  59.5 7.8 %copy-start.20 = (bf16[128,1280]{1,0:T(8,128)(2,1)}, bf16[128,1280]{1,0:T(8,128)(2,1)S(1)}, u32[]{:S(2)}) copy-start(bf16[128,1280]{1,0:T(8,128)(2,1)S(1)} %collective-permute-done.5) | copy-start | bytes 983044
  59.5 7.8 %collective-permute-start.6 = (bf16[128,1280]{1,0:T(8,128)(2,1)S(1)}, bf16[128,1280]{1,0:T(8,128)(2,1)}, u32[]{:S(2)}, u32[]{:S(2)}) collective-permute-start(bf16[128,1280]{1,0:T(8,128)(2,1)S(1)} %collective-permute-done.5), channel_id=1, source_target_pairs={{0,1},{1,2},{2,3},{3,4},{4,5},{5,6},{6,7},{7,8},{8,9},{9,10},{10,1... | collective-permute-start | bytes 983048 | tf_op jit(solution)/shard_map/ppermute | solution.py:133
  60.1 8.1 %collective-permute-start.13 = (bf16[128,1280]{1,0:T(8,128)(2,1)}, bf16[128,1280]{1,0:T(8,128)(2,1)}, u32[]{:S(2)}, u32[]{:S(2)}) collective-permute-start(bf16[128,1280]{1,0:T(8,128)(2,1)} %collective-permute-done.12), channel_id=1, source_target_pairs={{0,15},{1,0},{2,1},{3,2},{4,3},{5,4},{6,5},{7,6},{8,7},{9,8},{10,9... | collective-permute-start | bytes 983048 | tf_op jit(solution)/shard_map/ppermute | solution.py:135
  67.4 8.0 %collective-permute-start.7 = (bf16[128,1280]{1,0:T(8,128)(2,1)}, bf16[128,1280]{1,0:T(8,128)(2,1)}, u32[]{:S(2)}, u32[]{:S(2)}) collective-permute-start(bf16[128,1280]{1,0:T(8,128)(2,1)} %collective-permute-done.6), channel_id=1, source_target_pairs={{0,1},{1,2},{2,3},{3,4},{4,5},{5,6},{6,7},{7,8},{8,9},{9,10},{10,1... | collective-permute-start | bytes 983048 | tf_op jit(solution)/shard_map/ppermute | solution.py:133
  67.4 14.5 %copy-start.13 = (bf16[128,1280]{1,0:T(8,128)(2,1)S(1)}, bf16[128,1280]{1,0:T(8,128)(2,1)}, u32[]{:S(2)}) copy-start(bf16[128,1280]{1,0:T(8,128)(2,1)} %copy-done.12) | copy-start | bytes 983044
  67.4 14.5 %copy-start.15 = (bf16[128,1280]{1,0:T(8,128)(2,1)S(1)}, bf16[128,1280]{1,0:T(8,128)(2,1)}, u32[]{:S(2)}) copy-start(bf16[128,1280]{1,0:T(8,128)(2,1)} %copy-done.14) | copy-start | bytes 983044
  68.3 15.7 %collective-permute-start.14 = (bf16[128,1280]{1,0:T(8,128)(2,1)}, bf16[128,1280]{1,0:T(8,128)(2,1)S(1)}, u32[]{:S(2)}, u32[]{:S(2)}) collective-permute-start(bf16[128,1280]{1,0:T(8,128)(2,1)} %collective-permute-done.13), channel_id=1, source_target_pairs={{0,15},{1,0},{2,1},{3,2},{4,3},{5,4},{6,5},{7,6},{8,7},{9,8},{10,9... | collective-permute-start | bytes 983048 | tf_op jit(solution)/shard_map/ppermute | solution.py:135
  80.4 5.6 copy-start.21
  81.4 4.6 copy-start.19
  81.5 4.6 copy-start.17
  81.5 4.6 copy-start.11
  88.6 4.0 copy-start.32
  104.1 129.2 %copy-start.4 = (bf16[4,1,512,80]{3,2,1,0:T(8,128)(2,1)}, bf16[4,1,512,80]{3,2,1,0:T(8,128)(2,1)S(1)}, u32[]{:S(2)}) copy-start(bf16[4,1,512,80]{3,2,1,0:T(8,128)(2,1)S(1)} %get-tuple-element.373) | copy-start | bytes 983044
  109.9 81.7 %copy-start.35 = (f32[128,2]{0,1:T(2,128)S(1)}, f32[128,2]{0,1:T(2,128)}, u32[]{:S(2)}) copy-start(f32[128,2]{0,1:T(2,128)} %param.15) | copy-start | bytes 3076
  109.9 118.6 %all-gather.8.cloned.1.call-start = ((), (), s32[]{:S(2)}) async-start(), calls=%async_computation.8 | async-start | bytes 2785280 | tf_op jit(solution)/shard_map/all_gather | solution.py:181
  191.6 78.4 %all-gather.10.cloned.1.call-start = ((), (), s32[]{:S(2)}) async-start(), calls=%async_computation.9 | async-start | bytes 2785280 | tf_op jit(solution)/shard_map/all_gather | solution.py:208
  207.9 197.5 %all-reduce.9.cloned.1.call-start = ((), (), s32[]{:S(2)}) async-start(), calls=%async_computation.12 | async-start | bytes 10485760
  275.2 3.1 copy-start.8
  275.2 3.1 copy-start.23
  278.3 3.1 copy-start.38
  281.3 152.3 %copy-start.9 = (bf16[128,1280]{1,0:T(8,128)(2,1)S(1)}, bf16[128,1280]{1,0:T(8,128)(2,1)}, u32[]{:S(2)}) copy-start(bf16[128,1280]{1,0:T(8,128)(2,1)} %param.14) | copy-start | bytes 983044
  281.4 153.7 %copy-start.37 = (u32[256]{0:T(256)S(1)}, u32[256]{0:T(256)}, u32[]{:S(2)}) copy-start(u32[256]{0:T(256)} %constant.106) | copy-start | bytes 3076
  281.4 154.9 %copy-start.26 = (bf16[16,16,2,2,320]{4,1,3,0,2:T(8,128)(2,1)S(1)}, bf16[16,16,2,2,320]{4,1,3,0,2:T(8,128)(2,1)}, u32[]{:S(2)}) copy-start(bf16[16,16,2,2,320]{4,1,3,0,2:T(8,128)(2,1)} %copy-done.25) | copy-start | bytes 1966084
  407.8 13.7 %all-to-all-start.3 = ((bf16[16,2,2,1280]{3,2,1,0:T(2,128)(2,1)}), bf16[16,2,2,1280]{3,2,1,0:T(2,128)(2,1)S(1)}, u32[]{:S(2)}, u32[]{:S(2)}) async-start(bf16[16,2,2,1280]{3,2,1,0:T(2,128)(2,1)} %copy.57), calls=%async_computation.4 | async-start | bytes 327680 | tf_op jit(solution)/shard_map/all_to_all | solution.py:106
  421.6 11.6 %all-to-all-start.1 = ((bf16[16,2,2,1280]{3,2,1,0:T(2,128)(2,1)}), bf16[16,2,2,1280]{3,2,1,0:T(2,128)(2,1)S(1)}, u32[]{:S(2)}, u32[]{:S(2)}) async-start(bf16[16,2,2,1280]{3,2,1,0:T(2,128)(2,1)} %copy.54), calls=%async_computation.2 | async-start | bytes 327680 | tf_op jit(solution)/shard_map/all_to_all | solution.py:106
  426.7 49.2 %all-gather.6.cloned.1.call-start = ((), (), s32[]{:S(2)}) async-start(), calls=%async_computation.7 | async-start | bytes 5570560 | tf_op jit(solution)/shard_map/all_gather | solution.py:227
  433.6 42.4 %copy-start.7 = (bf16[10,8,4,512]{3,1,2,0:T(8,128)(2,1)S(1)}, bf16[10,8,4,512]{3,1,2,0:T(8,128)(2,1)}, u32[]{:S(2)}) copy-start(bf16[10,8,4,512]{3,1,2,0:T(8,128)(2,1)} %copy-done.6) | copy-start | bytes 983044
  435.0 137.1 %all-reduce.7.cloned.1.call-start = ((), (), s32[]{:S(2)}) async-start(), calls=%async_computation.11 | async-start | bytes 409600
  440.3 40.2 %copy-start.22 = (bf16[1,80,1280]{2,1,0:T(8,128)(2,1)S(1)}, bf16[1,80,1280]{2,1,0:T(8,128)(2,1)}, u32[]{:S(2)}) copy-start(bf16[1,80,1280]{2,1,0:T(8,128)(2,1)} %param.19) | copy-start | bytes 614404
  480.2 5.5 copy-start.28
  480.2 173.1 %reduce-scatter.14.cloned.1.call-start = ((), (), s32[]{:S(2)}) async-start(), calls=%async_computation.10 | async-start | bytes 696320
  485.7 3.3 copy-start.30
  490.7 3.1 copy-start.3
  496.6 3.3 copy-start.30
  501.7 3.1 copy-start.3
  504.7 3.0 copy-start.29
  504.7 3.0 copy-start.31
  507.7 3.3 copy-start.30
  512.8 3.1 copy-start.3
  515.9 3.0 copy-start.29
  515.9 3.0 copy-start.31
  518.9 3.3 copy-start.30
  524.0 3.1 copy-start.3
  527.0 3.0 copy-start.29
  527.0 3.0 copy-start.31
  532.2 5.2 copy-start.24
  537.4 117.6 %copy-start.1 = (bf16[2,1280,320]{1,2,0:T(8,128)(2,1)S(1)}, bf16[2,1280,320]{1,2,0:T(8,128)(2,1)}, u32[]{:S(2)}) copy-start(bf16[2,1280,320]{1,2,0:T(8,128)(2,1)} %param.20) | copy-start | bytes 4915204
  (17 other events, 27.2 us)
Sparse Core Ops, SparseCore 0:
  110.1 65.4 reduce-scatter.11
  191.7 36.8 all-gather.7
  231.0 38.9 all-gather.9
  281.5 123.9 all-reduce.8
  435.1 40.8 all-gather.5
  480.3 91.7 all-reduce.6
  575.9 77.3 reduce-scatter.13
